TPU v7x, 128 devices: a whole 4x4x4 slice. The times are simulated.
128 devices in a mesh: chan: 8 (over z, x_lo), tm: 16 (over y, x_hi, core).
Axes of the slice: x: 4 (x_hi: 2, x_lo: 2; x = x_hi * 2 + x_lo), y: 4, z: 4, core: 2. Of those that a mesh axis runs over, the one named last changes fastest.
Arguments:
- recording: bfloat16 [4096, 240000], P('chan', 'tm'), may hold values from -6 to 6
- offsets: int32 [32], replicated, may hold values from 0 to 3749, as said below
- band_bins: int32 [20], replicated, may hold values from 61 to 300
- dead_flags: int32 [4096], P('chan'), may hold values 0 or 1
Outputs:
- stacks: bfloat16 [2, 20, 4096, 4096], P(None, None, 'tm', 'chan')
Inputs may be any that keep to these rules, and one draw needn't show every extreme that they name: `offsets`: every window's offset is drawn afresh; the last window of some block of 2 consecutive windows has the largest offset.
All inputs are finite; a program needn't handle non-finite values. No bound on the sum of `dead_flags` on one device may be relied on, other than what follows from the above.
Results may differ from a plain program's by a relative error of at most 0.0063.
Values may be sent and summed in bfloat16 or wider, within the bound.
A program may use at most 128 MiB of HBM per device.

v0:
```python
import math

import jax
import jax.numpy as jnp
from jax import lax
from jax.sharding import Mesh
from jax.sharding import PartitionSpec as P

L = 15000
NB = 20
TM = ("tm_0", "tm_1", "tm_2")


TWO_PI = 2.0 * math.pi
FLOOR = 0.7


def shifted(block, axis, distance):
    devices = range(lax.axis_size(axis))
    route = [(i - distance, i) for i in devices if i - distance in devices]
    return lax.ppermute(block, axis, route)


def laid_out(blocks, dim):
    blocks = jnp.moveaxis(blocks, 0, dim)
    dims = blocks.shape
    return blocks.reshape(*dims[:dim], dims[dim] * dims[dim + 1], *dims[dim + 2 :])


def sent_to_all(shard, axis):
    copies = jnp.broadcast_to(shard, (lax.axis_size(axis), *shard.shape))
    return lax.all_to_all(copies, axis, split_axis=0, concat_axis=0, tiled=True)


def gather_directly(shard, axis, dim):
    return laid_out(sent_to_all(shard, axis), dim)


def in_blocks(shard, dim, size):
    dims = shard.shape
    blocks = shard.reshape(*dims[:dim], size, dims[dim] // size, *dims[dim + 1 :])
    return jnp.moveaxis(blocks, dim, 0)


def exchange_in_order(blocks, axes, order):
    inside = blocks.shape[1:]
    whole = blocks.reshape(*(lax.axis_size(a) for a in axes), *inside)
    for k in order:
        whole = lax.all_to_all(whole, axes[k], k, k, tiled=True)
    return whole.reshape(-1, *inside)


def exchange_by_chip(shard, groups, order, split_dim, concat_dim):
    size = lax.axis_size(groups[0]) * lax.axis_size(groups[1])
    blocks = in_blocks(shard, split_dim, size)
    return laid_out(exchange_in_order(blocks, groups, order), concat_dim)


def phase_table(band_bins, shifts, span_len, length):
    position = (
        lax.broadcasted_iota(jnp.int32, (shifts.shape[0], 1, span_len), 2) - shifts[:, None, None]
    )
    inside = (position >= 0) & (position < length)
    lag_index = jnp.where(inside, position, 0)
    turn_index = band_bins[None, :, None] * lag_index % length
    angles = turn_index.astype(jnp.float32) * (TWO_PI / length)
    norm_scale = 1.0 / math.sqrt(length)
    cosine = jnp.where(inside, jnp.cos(angles) * norm_scale, 0.0)
    sine_part = jnp.where(inside, -jnp.sin(angles) * norm_scale, 0.0)
    dft_table = jnp.concatenate([cosine, sine_part], axis=1).astype(jnp.bfloat16)
    weights = inside[:, 0, :].astype(jnp.float32)
    return (dft_table, weights)


def partial_spectra(samples, dft_table, weights):
    raw_spectra = jnp.einsum("wks,cs->wkc", dft_table, samples, preferred_element_type=jnp.float32)
    squares = samples.astype(jnp.float32)
    squares = squares * squares
    energy = jnp.einsum("ws,cs->wc", weights, squares, precision=lax.Precision.HIGHEST)
    return (raw_spectra, energy)


def shards(recording, offsets, band_bins, dead_flags):
    channels, block_len = recording.shape
    length = L
    hop_size = length // 2
    rim_width = hop_size + hop_size // 2
    windows = block_len // hop_size
    tm_count = lax.axis_size(TM)
    tm_index = lax.axis_index(TM)
    own_offsets = lax.dynamic_slice_in_dim(offsets, tm_index * windows, windows)
    starts = jnp.arange(windows, dtype=jnp.int32) * hop_size + own_offsets
    dft_table, weights = phase_table(band_bins, starts, block_len, length)
    raw_spectra, energy = partial_spectra(recording, dft_table, weights)
    before = lax.dynamic_slice_in_dim(offsets, jnp.maximum(tm_index - 1, 0) * windows, windows)
    back_starts = jnp.arange(windows, dtype=jnp.int32) * hop_size + before - block_len
    back_table, back_weights = phase_table(band_bins, back_starts, rim_width, length)
    back_raw, back_energy = partial_spectra(recording[:, :rim_width], back_table, back_weights)
    more_raw, more_energy = shifted((back_raw, back_energy), TM, -1)
    raw_spectra = raw_spectra + more_raw
    energy = energy + more_energy
    spectra = raw_spectra / jnp.sqrt(energy / length + 1e-06)[:, None, :]
    level = jnp.mean(spectra * spectra, axis=1) * 2.0
    alive = (1 - dead_flags).astype(jnp.float32)
    factor = alive[None, :] / jnp.sqrt(jnp.maximum(level, FLOOR))
    white = (spectra * factor[:, None, :]).astype(jnp.bfloat16).reshape(windows, 2, NB, channels)
    rows_all = lax.all_gather(white, TM, axis=0, tiled=True)
    every_chan = gather_directly(white, "chan", 3)
    cols_all = exchange_by_chip(every_chan, (("tm_0", "tm_1"), "tm_2"), (1, 0), 3, 0)
    flipped = jnp.stack([-cols_all[:, 1], cols_all[:, 0]], axis=1)
    both_cols = jnp.stack([cols_all, flipped], axis=0)
    stacked = jnp.einsum(
        "swpbj,wpbi->sbji", both_cols, rows_all, preferred_element_type=jnp.float32
    )
    stack_scale = 1.0 / math.sqrt(windows * tm_count)
    return (stacked * stack_scale).astype(jnp.bfloat16)


def solution(mesh):
    torus = Mesh(
        mesh.devices.reshape(mesh.shape["chan"], 4, 2, 2), ("chan", "tm_0", "tm_1", "tm_2")
    )
    in_specs = (P("chan", TM), P(), P(), P("chan"))
    out_specs = P(None, None, TM, "chan")
    return jax.shard_map(
        shards, mesh=torus, in_specs=in_specs, out_specs=out_specs, check_vma=False
    )
```

profile of v0, /device:TPU:1, one launch (start us, length us, event | category | flops | bytes accessed | tf_op | source)
XLA Modules:
  0.0 144.6 jit_solution(7098418087072442390)
XLA Ops:
  6.5 0.0 all-gather.2.cloned.1.call-start
  6.5 0.8 dynamic-slice_add_fusion
  7.3 0.0 copy-start.1
  7.3 0.0 copy-start
  7.3 12.1 %fusion.3 = f32[2,512]{1,0:T(2,128)S(1)} fusion(bf16[512,15000]{0,1:T(8,128)(2,1)} %param.4, s32[2]{0:T(128)S(1)} %get-tuple-element.12), kind=kOutput, calls=%fused_computation.3 | convolution fusion | flops 149850000 | bytes 11530248 | tf_op jit(solution)/shard_map/ws,cs->wc/dot_general | solution.py:79
  19.4 3.3 %collective-permute-start.1 = (f32[2,512]{1,0:T(2,128)S(1)}, f32[2,512]{1,0:T(2,128)S(1)}, u32[]{:S(2)}, u32[]{:S(2)}) collective-permute-start(f32[2,512]{1,0:T(2,128)S(1)} %fusion.3), channel_id=1, source_target_pairs={{1,0},{2,1},{3,2},{4,3},{5,4},{6,5},{7,6},{8,7},{9,8},{10,9},{11,1... | collective-permute-start | bytes 12296 | tf_op jit(solution)/shard_map/ppermute | solution.py:21
  22.7 0.2 compare_and_fusion.1
  22.9 0.1 fusion.57
  23.0 0.0 copy-done.1
  23.0 9.4 %select_convert_fusion.3 = (bf16[2,20,11250]{2,1,0:T(8,128)(2,1)S(1)}, bf16[2,20,11250]{2,1,0:T(8,128)(2,1)S(1)}) fusion(s32[2,11250]{1,0:T(2,128)S(1)} %fusion.57, s32[20]{0:T(128)S(1)} %copy-done.1, pred[2,11250]{1,0:T(4,128)(4,1)S(1)} %compare_and_fusion.1), kind=kLoop, calls=%fused_computation.31 | loop fusion | flops 7200000 | bytes 1912580 | tf_op jit(solution)/shard_map/convert
  32.5 0.0 copy-done
  32.5 1.8 %fusion.9 = f32[2,40,512]{2,1,0:T(8,128)S(1)} fusion(bf16[512,15000]{0,1:T(8,128)(2,1)S(1)} %copy-done, bf16[2,20,11250]{2,1,0:T(8,128)(2,1)S(1)} %get-tuple-element.10, bf16[2,20,11250]{2,1,0:T(8,128)(2,1)S(1)} %get-tuple-element.9), kind=kOutput, calls=%fused_computation.10 | convolution fusion | flops 925200000 | bytes 13852672 | tf_op jit(solution)/shard_map/wks,cs->wkc/dot_general | solution.py:76
  34.2 0.0 copy-start.2
  34.3 1.9 %collective-permute-start = (f32[2,40,512]{2,1,0:T(8,128)S(1)}, f32[2,40,512]{2,1,0:T(8,128)S(1)}, u32[]{:S(2)}, u32[]{:S(2)}) collective-permute-start(f32[2,40,512]{2,1,0:T(8,128)S(1)} %fusion.9), channel_id=1, source_target_pairs={{1,0},{2,1},{3,2},{4,3},{5,4},{6,5},{7,6},{8,7},{9,8},{10,9},{11,1... | collective-permute-start | bytes 491528 | tf_op jit(solution)/shard_map/ppermute | solution.py:21
  36.2 0.2 compare_and_fusion
  36.4 0.2 fusion.56
  36.5 12.7 %select_convert_fusion.1 = (bf16[2,20,15000]{2,1,0:T(8,128)(2,1)S(1)}, bf16[2,20,15000]{2,1,0:T(8,128)(2,1)S(1)}) fusion(s32[2,15000]{1,0:T(2,128)S(1)} %fusion.56, s32[20]{0:T(128)S(1)} %copy-done.1, pred[2,15000]{1,0:T(4,128)(4,1)S(1)} %compare_and_fusion), kind=kLoop, calls=%fused_computation.20 | loop fusion | flops 9600000 | bytes 2550080 | tf_op jit(solution)/shard_map/convert.2
  49.2 0.0 copy-done.2
  49.3 0.0 collective-permute-done.1
  49.3 11.9 %fusion.48 = f32[2,512]{1,0:T(2,128)S(1)} fusion(f32[2,512]{1,0:T(2,128)S(1)} %collective-permute-done.1, bf16[512,15000]{0,1:T(8,128)(2,1)S(1)} %copy-done, s32[2]{0:T(128)S(1)} %get-tuple-element.11), kind=kOutput, calls=%fused_computation.47 | convolution fusion | flops 199803072 | bytes 15368200 | tf_op jit(solution)/shard_map/ws,cs->wc/dot_general | solution.py:79
  61.2 0.0 collective-permute-done
  61.2 2.5 %multiply_reduce_fusion = (f32[2,512]{1,0:T(2,128)S(1)}, f32[2,40,512]{2,1,0:T(8,128)S(1)}) fusion(f32[2,512]{1,0:T(2,128)S(1)} %fusion.48, f32[2,40,512]{2,1,0:T(8,128)S(1)} %collective-permute-done, bf16[512,15000]{0,1:T(8,128)(2,1)S(1)} %copy-done, bf16[2,20,15000]{2,1,0:T(8,128)(2,1)S(1)} %get-tuple-element.8, ...), kind=kOutput, calls=%fused_computation.54 | convolution fusion | flops 1233762816 | bytes 18095872 | tf_op jit(solution)/shard_map/wks,cs->wkc/dot_general | solution.py:76
  63.8 0.1 copy.22
  63.9 0.7 copy.23
  64.6 0.0 all-gather.2.cloned.1.call-update
  64.6 1.2 broadcast_in_dim.50
  65.8 17.9 %all_to_all.15 = bf16[8,2,2,20,512]{4,2,3,1,0:T(2,128)(2,1)S(1)} all-to-all(bf16[8,2,2,20,512]{4,2,3,1,0:T(2,128)(2,1)S(1)} %broadcast_in_dim.50), channel_id=1, replica_groups=mesh['chan'=8,'tm_0'=4,'tm_1'=2,'tm_2'=2] {'chan'}, dimensions={0} | all-to-all | bytes 1310720 | tf_op jit(solution)/shard_map/all_to_all | solution.py:32
  83.8 0.4 copy.25
  84.1 0.2 reshape_reshape.6
  84.4 0.2 reshape.106
  84.6 0.7 copy.26
  85.3 3.9 %all_to_all.16 = bf16[8,2,2,2,20,256]{5,2,0,3,4,1:T(2,128)(2,1)S(1)} all-to-all(bf16[8,2,2,2,20,256]{5,2,0,3,4,1:T(2,128)(2,1)S(1)} %copy.26), channel_id=1, replica_groups=mesh['chan'=8,'tm_0'=4,'tm_1'=2,'tm_2'=2] {'tm_2'}, dimensions={1} | all-to-all | bytes 1310720 | tf_op jit(solution)/shard_map/all_to_all | solution.py:49
  89.2 0.5 copy.27
  89.7 24.6 %all_to_all.17 = bf16[8,2,2,2,20,256]{5,2,1,3,4,0:T(2,128)(2,1)S(1)} all-to-all(bf16[8,2,2,2,20,256]{5,2,1,3,4,0:T(2,128)(2,1)S(1)} %copy.27), channel_id=1, replica_groups=mesh['chan'=8,'tm_0'=4,'tm_1'=2,'tm_2'=2] {'tm_0','tm_1'}, dimensions={0} | all-to-all | bytes 1310720 | tf_op jit(solution)/shard_map/all_to_all | solution.py:49
  114.2 0.7 copy.28
  114.9 0.3 reshape_reshape.7
  115.2 0.2 stack_reshape_reshape.3
  115.5 0.1 maximum_bitcast_fusion
  115.6 1.3 all-gather.2.cloned.1.call-done
  116.9 7.2 %fusion.11 = bf16[2,20,256,512]{2,3,0,1:T(8,128)(2,1)} fusion(bf16[1,32,2,20,256]{4,1,2,0,3:T(8,128)(2,1)S(1)} %maximum_bitcast_fusion, bf16[1,32,2,20,256]{4,1,2,0,3:T(8,128)(2,1)S(1)} %stack_reshape_reshape.3, bf16[32,2,20,512,1]{3,1,2,0,4:T(2,128)(2,1)} %bitcast.40), kind=kOutput, calls=%fused_computation.12 | convolution fusion | flops 684195840 | bytes 13107200 | tf_op jit(solution)/shard_map/swpbj,wpbi->sbji/dot_general | solution.py:112
  124.0 13.7 %copy.31 = bf16[2,20,256,512]{3,2,1,0:T(8,128)(2,1)} copy(bf16[2,20,256,512]{2,3,0,1:T(8,128)(2,1)} %fusion.11) | data formatting | bytes 20971520 | tf_op jit(solution)/shard_map/convert_element_type | solution.py:116
  (4 shorter events, 0.1 us)
Async XLA Ops:
  6.5 110.3 %all-gather.2.cloned.1.call-start = ((), (), s32[]{:S(2)}) async-start(), calls=%async_computation.3 | async-start | bytes 1392640 | tf_op jit(solution)/shard_map/all_gather | solution.py:107
  7.3 15.7 %copy-start.1 = (s32[20]{0:T(128)S(1)}, s32[20]{0:T(128)}, u32[]{:S(2)}) copy-start(s32[20]{0:T(128)} %param.6) | copy-start | bytes 244
  7.3 25.1 %copy-start = (bf16[512,15000]{0,1:T(8,128)(2,1)S(1)}, bf16[512,15000]{0,1:T(8,128)(2,1)}, u32[]{:S(2)}) copy-start(bf16[512,15000]{0,1:T(8,128)(2,1)} %param.4) | copy-start | bytes 46080004
  19.4 29.9 %collective-permute-start.1 = (f32[2,512]{1,0:T(2,128)S(1)}, f32[2,512]{1,0:T(2,128)S(1)}, u32[]{:S(2)}, u32[]{:S(2)}) collective-permute-start(f32[2,512]{1,0:T(2,128)S(1)} %fusion.3), channel_id=1, source_target_pairs={{1,0},{2,1},{3,2},{4,3},{5,4},{6,5},{7,6},{8,7},{9,8},{10,9},{11,1... | collective-permute-start | bytes 12296 | tf_op jit(solution)/shard_map/ppermute | solution.py:21
  34.2 15.0 %copy-start.2 = (s32[512]{0:T(512)S(1)}, s32[512]{0:T(512)}, u32[]{:S(2)}) copy-start(s32[512]{0:T(512)} %param.7) | copy-start | bytes 6148
  34.3 26.9 %collective-permute-start = (f32[2,40,512]{2,1,0:T(8,128)S(1)}, f32[2,40,512]{2,1,0:T(8,128)S(1)}, u32[]{:S(2)}, u32[]{:S(2)}) collective-permute-start(f32[2,40,512]{2,1,0:T(8,128)S(1)} %fusion.9), channel_id=1, source_target_pairs={{1,0},{2,1},{3,2},{4,3},{5,4},{6,5},{7,6},{8,7},{9,8},{10,9},{11,1... | collective-permute-start | bytes 491528 | tf_op jit(solution)/shard_map/ppermute | solution.py:21
Sparse Core Ops, SparseCore 0:
  64.7 52.1 all-gather.1
where the time goes:
time: 145 us
  blocking collectives  46.4 us (32%)
  matrix products  35.5 us (24%)
  other arithmetic  23.7 us (16%)
  local copies, waits for them, and re-layouts  18.9 us (13%)
  between operations  13.6 us (9%)
  starting transfers between devices  5.21 us (4%)
    all_to_all x2, blocking collectives, exchange_in_order(): whole = lax.all_to_all(whole, axes[k], k, k, tiled=True)  28.5 us
    dot_general x2, matrix products, partial_spectra(): jnp.einsum('ws,cs->wc', weights, squares, precision=lax.Precision.HIGHEST)  24 us
    another operation x2, other arithmetic  22.1 us
    all_to_all x1, blocking collectives, sent_to_all(): return lax.all_to_all(copies, axis, split_axis=0, concat_axis=0, tiled=True)  17.9 us
    convert_element_type x1, local copies, waits for them, and re-layouts, shards(): return (stacked * stack_scale).astype(jnp.bfloat16)  13.7 us
    dot_general x1, matrix products, shards(): jnp.einsum('swpbj,wpbi->sbji', both_cols, rows_all, preferred_element_typ...  7.18 us
    ppermute x2, starting transfers between devices, shifted(): return lax.ppermute(block, axis, route)  5.21 us
    dot_general x2, matrix products, partial_spectra(): jnp.einsum('wks,cs->wkc', dft_table, samples, preferred_element_type=jnp....  4.33 us
  transfers between devices with their start and end apart: 3, of which 1 were waited for; matrix products, arithmetic and copies ran while one was open for 28% of the time, Pallas kernels for 0%

commit v1 on v0

v1 whole, which is shorter than its diff:
```python
import functools
import math

import jax
import jax.numpy as jnp
from jax import lax
from jax.experimental import pallas as pl
from jax.experimental.pallas import tpu as pltpu
from jax.sharding import PartitionSpec as P

L = 15000
NB = 20
HOP = L // 2
TWO_PI = 2.0 * math.pi
FLOOR = 0.7
WIN = 32
STEP = 1024
CHUNKS = 15
ROWS = 40
F32 = jnp.float32
BF16 = jnp.bfloat16


def bin_rows(bins):
    row = lax.broadcasted_iota(jnp.int32, (24, 128), 0)
    out = jnp.zeros((24, 128), jnp.int32)
    for b in range(NB):
        hit = row == b
        if b >= 16:
            hit = hit | (row == b + 4)
        out = jnp.where(hit, bins[b], out)
    return out.astype(F32)


def turned(turns):
    whole = jnp.floor(turns * (1.0 / L))
    rest = turns - whole * float(L)
    rest = jnp.where(rest < 0.0, rest + float(L), rest)
    rest = jnp.where(rest >= float(L), rest - float(L), rest)
    angle = rest * (TWO_PI / L)
    return jnp.cos(angle), jnp.sin(angle)


def start_state(bins, first):
    lane = lax.broadcasted_iota(jnp.int32, (24, 128), 1)
    row = lax.broadcasted_iota(jnp.int32, (24, 128), 0)
    place = (lane + (first + L)).astype(F32)
    quarter = jnp.where(row >= 20, float(L // 4), 0.0)
    cosine, sine = turned(bins * place + quarter)
    scale = 1.0 / math.sqrt(L)
    return cosine * scale, -sine * scale


def turn_on(state, step):
    v, q = state
    c, s = step
    return v * c + q * s, q * c - v * s


def table_rows(state, keep):
    v, q = state
    rows = jnp.concatenate([v[:16], q[:16], v[16:]], axis=0)
    return rows if keep is None else jnp.where(keep, rows, 0.0)


def local_sums(x_hbm, offs, bins_ref, part, xbuf, tab, sems):
    t = lax.axis_index("tm")

    def chunk_copy(g):
        rows = STEP if isinstance(g, jax.Array) or g < CHUNKS - 1 else L - STEP * (CHUNKS - 1)
        at = pl.ds(pl.multiple_of(g * STEP, STEP), rows)
        return pltpu.make_async_copy(x_hbm.at[at], xbuf.at[at], sems.at[g])

    tail = (L // 16) * 16
    xbuf[pl.ds(tail, CHUNKS * STEP - tail)] = jnp.zeros((CHUNKS * STEP - tail, 512), BF16)
    for g in range(CHUNKS):
        chunk_copy(g).start()

    before = 2 * jnp.maximum(t - 1, 0)
    off0, off1 = offs[2 * t], offs[2 * t + 1]
    boff0, boff1 = offs[before], offs[before + 1]
    a0, a1 = off0, HOP + off1
    e0, e1 = boff0, HOP + boff1

    bins = bin_rows(bins_ref)
    step = turned(bins * 128.0)
    part[...] = jnp.zeros_like(part)

    low = jnp.zeros((16, STEP), jnp.int32)
    high = jnp.zeros((16, STEP), jnp.int32)
    row = lax.broadcasted_iota(jnp.int32, (16, STEP), 0)
    for r, (lo, hi) in enumerate(((a0, L), (a1, L), (0, e0), (0, e1))):
        low = jnp.where(row == r, lo, low)
        high = jnp.where(row == r, hi, high)
    inner = lax.broadcasted_iota(jnp.int32, (16, STEP), 1)
    lane = lax.broadcasted_iota(jnp.int32, (ROWS, 128), 1)

    def chunk(g, states, slots):
        states = list(states)
        for k in range(STEP // 128):
            place = lane + (g * STEP + k * 128)
            rows = []
            for n, (_, limit) in enumerate(slots):
                keep = None
                if limit is not None:
                    keep = place >= limit[1] if limit[0] else place < limit[1]
                rows.append(table_rows(states[n], keep))
                states[n] = turn_on(states[n], step)
            if len(slots) == 3:
                rows.append(jnp.zeros((8, 128), F32))
            made = jnp.concatenate(rows, axis=0).astype(BF16)
            tab[0 : made.shape[0], k * 128 : (k + 1) * 128] = made
        chunk_copy(g).wait()
        height = 128 if len(slots) == 3 else 80
        x = xbuf[pl.ds(pl.multiple_of(g * STEP, STEP), STEP), :]
        raw = jnp.dot(tab[0:height, :], x, preferred_element_type=F32)
        place = inner + g * STEP
        mask = jnp.where((place >= low) & (place < high), 1.0, 0.0).astype(BF16)
        square = jnp.dot(mask, x * x, preferred_element_type=F32)
        for n, (target, _) in enumerate(slots):
            half, w = target
            part[half, w * ROWS : (w + 1) * ROWS] += raw[n * ROWS : (n + 1) * ROWS]
        part[0, 80:88] += square[0:8]
        return tuple(states)

    own0, own1, back0, back1 = (0, 0), (0, 1), (1, 0), (1, 1)
    s_own0 = start_state(bins, -a0)
    s_back0 = start_state(bins, L - e0)
    s_back1 = start_state(bins, L - e1)
    s_own1 = start_state(bins, 7 * STEP - a1)

    slots = ((own0, (True, a0)), (back1, None), (back0, (False, e0)))
    s_own0, s_back1, _ = lax.fori_loop(
        0, 4, lambda g, s: chunk(g, s, slots), (s_own0, s_back1, s_back0)
    )
    slots1 = ((own0, None), (back1, None))
    s_own0, s_back1 = lax.fori_loop(4, 7, lambda g, s: chunk(g, s, slots1), (s_own0, s_back1))
    slots2 = ((own0, None), (back1, (False, e1)), (own1, (True, a1)))
    s_own0, _, s_own1 = lax.fori_loop(
        7, 11, lambda g, s: chunk(g, s, slots2), (s_own0, s_back1, s_own1)
    )
    slots3 = ((own0, None), (own1, None))
    states = lax.fori_loop(11, 14, lambda g, s: chunk(g, s, slots3), (s_own0, s_own1))
    chunk(14, states, slots3)
    part[1, 80:82] = part[0, 82:84]


def local_call(x, offsets, band_bins):
    return pl.pallas_call(
        local_sums,
        out_shape=jax.ShapeDtypeStruct((2, 88, 512), F32),
        in_specs=[
            pl.BlockSpec(memory_space=pl.ANY),
            pl.BlockSpec(memory_space=pltpu.SMEM),
            pl.BlockSpec(memory_space=pltpu.SMEM),
        ],
        out_specs=pl.BlockSpec(memory_space=pltpu.VMEM),
        scratch_shapes=[
            pltpu.VMEM((CHUNKS * STEP, 512), BF16),
            pltpu.VMEM((128, STEP), BF16),
            pltpu.SemaphoreType.DMA((CHUNKS,)),
        ],
        compiler_params=pltpu.CompilerParams(vmem_limit_bytes=48 << 20),
        name="local_sums",
    )(x, offsets, band_bins)


def whitened(total, dead):
    alive = 1.0 - dead.astype(F32)
    out = []
    for w in range(2):
        raw = total[w * ROWS : (w + 1) * ROWS]
        energy = total[80 + w : 81 + w]
        spectra = raw / jnp.sqrt(energy / L + 1e-06)
        level = jnp.sum(spectra * spectra, axis=0, keepdims=True) * (1.0 / NB)
        out.append(spectra * (alive / jnp.sqrt(jnp.maximum(level, FLOOR))))
    return jnp.concatenate(out, axis=0).astype(BF16)


def regroup():
    d = lax.broadcasted_iota(jnp.int32, (80, 80), 0)
    s = lax.broadcasted_iota(jnp.int32, (80, 80), 1)
    p, w = (d >> 3) & 1, (d >> 2) & 1
    b = (d >> 4) * 4 + (d & 3)
    source = w * ROWS + jnp.where(b < 16, p * 16 + b, 32 + p * 4 + (b - 16))
    return jnp.where(s == source, 1.0, 0.0).astype(BF16)


def exchange(part, dead, gi, gj, back, send_sems, back_sems, i_sems, j_sems):
    c = lax.axis_index("chan")
    t = lax.axis_index("tm")
    z, xl = c // 2, c % 2
    y, xh, core = t // 4, (t // 2) % 2, t % 2
    sent = []

    def send(source, target, recv, device):
        copy = pltpu.make_async_remote_copy(
            src_ref=source,
            dst_ref=target,
            send_sem=send_sems.at[len(sent)],
            recv_sem=recv,
            device_id=device,
            device_id_type=pl.DeviceIdType.MESH,
        )
        copy.start()
        sent.append(copy)

    def block_of(yy, hi, k):
        return 4 * (yy % 4) + 2 * hi + k

    up, down = (c, block_of(y + 1, xh, core)), (c, block_of(y + 3, xh, core))
    across, other = (c, block_of(y, 1 - xh, core)), (c, block_of(y, xh, 1 - core))
    z_up, z_down = ((c + 2) % 8, t), ((c + 6) % 8, t)
    previous, following = (c, (t + 15) % 16), (c, (t + 1) % 16)

    barrier = pltpu.get_barrier_semaphore()
    sources = [up, down, across, other, z_up, z_down, following]
    sources += [(2 * y + xh, block_of(z + 2, hi, k)) for hi in range(2) for k in range(2)]
    for device in sources:
        pl.semaphore_signal(
            barrier, inc=1, device_id=device, device_id_type=pl.DeviceIdType.MESH
        )
    pl.semaphore_wait(barrier, len(sources))

    send(part.at[1], back, back_sems.at[0], previous)
    matrix = regroup()
    sent[0].wait_recv()
    more = jnp.where(t == 15, 0.0, back[...])
    white = whitened(part[0] + more, dead[...])
    ordered = jnp.dot(matrix, white, preferred_element_type=F32).astype(BF16)
    for h in range(2):
        gi[t, h] = ordered[:, h * 256 : (h + 1) * 256]

    def give(block, h, device):
        send(gi.at[block, h], gi.at[block, h], i_sems.at[block, h], device)

    def got(block, h):
        pltpu.make_async_copy(gi.at[block, h], gi.at[block, h], i_sems.at[block, h]).wait()

    def pass_j(q, s, device):
        send(gj.at[q, s], gj.at[q, s], j_sems.at[q, s], device)

    def got_j(q, s):
        pltpu.make_async_copy(gj.at[q, s], gj.at[q, s], j_sems.at[q, s]).wait()

    halves = range(2)
    for h in halves:
        give(t, h, across)
    for lo in halves:
        for h in halves:
            send(
                gi.at[t, h],
                gj.at[t // 2, core],
                j_sems.at[t // 2, core],
                (2 * ((y + 2) % 4) + lo, block_of(z, xl, h)),
            )
    for h in halves:
        give(t, h, up)
        give(t, h, down)
    for h in halves:
        give(t, h, other)

    near = block_of(y, 1 - xh, core)
    below, above = block_of(y + 3, xh, core), block_of(y + 1, xh, core)
    far = block_of(y + 2, xh, core)
    near_below, near_above = block_of(y + 3, 1 - xh, core), block_of(y + 1, 1 - xh, core)
    near_far = block_of(y + 2, 1 - xh, core)

    got(below, 0)
    give(below, 0, up)
    got(above, 1)
    give(above, 1, down)
    for h in halves:
        got(near, h)
        give(near, h, up)
        give(near, h, down)
    q_own = [2 * ((z + 2) % 4) + hi for hi in range(2)]
    q_low = [2 * ((z + 1) % 4) + hi for hi in range(2)]
    q_high = [2 * ((z + 3) % 4) + hi for hi in range(2)]
    q_far = [2 * z + hi for hi in range(2)]
    for q in q_own:
        for s in halves:
            got_j(q, s)
            pass_j(q, s, z_up)
            pass_j(q, s, z_down)
    got(below, 1)
    got(above, 0)
    for block in (below, above, near):
        for h in halves:
            give(block, h, other)
    got(near_below, 0)
    give(near_below, 0, up)
    got(near_above, 1)
    give(near_above, 1, down)
    for q_l, q_h in zip(q_low, q_high):
        got_j(q_l, 0)
        pass_j(q_l, 0, z_up)
        got_j(q_h, 1)
        pass_j(q_h, 1, z_down)
    got(near_below, 1)
    got(near_above, 0)
    for block in (near_below, near_above):
        for h in halves:
            give(block, h, other)
    for block in (far, near_far):
        for h in halves:
            got(block, h)
            give(block, h, other)
    for q_l, q_h in zip(q_low, q_high):
        got_j(q_l, 1)
        got_j(q_h, 0)
    for q in q_far:
        for s in halves:
            got_j(q, s)
    for yy in range(4):
        for hi in range(2):
            for h in halves:
                got(block_of(yy, hi, 1 - core), h)
    for copy in sent:
        copy.wait_send()


N_SENDS = 1 + 2 + 4 + 4 + 2 + 2 + 4 + 8 + 6 + 2 + 4 + 4 + 4


def exchange_call(part, dead):
    vmem = pl.BlockSpec(memory_space=pltpu.VMEM)
    return pl.pallas_call(
        exchange,
        out_shape=(
            jax.ShapeDtypeStruct((16, 2, 80, 256), BF16),
            jax.ShapeDtypeStruct((8, 2, 80, 256), BF16),
        ),
        in_specs=[vmem, vmem],
        out_specs=(vmem, vmem),
        scratch_shapes=[
            pltpu.VMEM((88, 512), F32),
            pltpu.SemaphoreType.DMA((N_SENDS,)),
            pltpu.SemaphoreType.DMA((1,)),
            pltpu.SemaphoreType.DMA((16, 2)),
            pltpu.SemaphoreType.DMA((8, 2)),
        ],
        compiler_params=pltpu.CompilerParams(collective_id=0, has_side_effects=True),
        name="exchange",
    )(part, dead)


def stack_group(gi, gj, out, lhs):
    xj = gj[...].reshape(16, 16, 256).astype(F32)
    flipped = jnp.concatenate([-xj[:, 8:], xj[:, :8]], axis=1)
    bin_of = lax.broadcasted_iota(jnp.int32, (256, 256), 1) & 3
    for s, rows in enumerate((xj, flipped)):
        turned_rows = rows.reshape(256, 256).T
        for b in range(4):
            at = (s * 4 + b) * 256
            lhs[at : at + 256] = jnp.where(bin_of == b, turned_rows, 0.0).astype(BF16)
    scale = 1.0 / math.sqrt(WIN)
    for h in range(2):
        right = gi[:, h].reshape(256, 256)
        for s in range(2):
            for b in range(4):
                at = (s * 4 + b) * 256
                made = jnp.dot(lhs[at : at + 256], right, preferred_element_type=F32)
                out[s, b, :, h * 256 : (h + 1) * 256] = (made * scale).astype(BF16)


def stack_call(gi, gj):
    return pl.pallas_call(
        stack_group,
        out_shape=jax.ShapeDtypeStruct((2, NB, 256, 512), BF16),
        grid=(5,),
        in_specs=[
            pl.BlockSpec((16, 2, 16, 256), lambda g: (0, 0, g, 0)),
            pl.BlockSpec((8, 2, 16, 256), lambda g: (0, 0, g, 0)),
        ],
        out_specs=pl.BlockSpec((2, 4, 256, 512), lambda g: (0, g, 0, 0)),
        scratch_shapes=[pltpu.VMEM((2048, 256), BF16)],
        name="stack",
    )(gi, gj)


def shards(recording, offsets, band_bins, dead_flags):
    part = local_call(recording.T, offsets, band_bins)
    gi, gj = exchange_call(part, dead_flags.reshape(1, -1))
    return stack_call(gi, gj)


def solution(mesh):
    return jax.shard_map(
        shards,
        mesh=mesh,
        in_specs=(P("chan", "tm"), P(), P(), P("chan")),
        out_specs=P(None, None, "tm", "chan"),
        check_vma=False,
    )
```

time: 145 us -> 51 us (0.35)
  Pallas kernels: 0 us -> 48.7 us
  blocking collectives: 46.4 us -> 0 us
  matrix products: 35.5 us -> 0 us
  other arithmetic: 23.7 us -> 0 us
  local copies, waits for them, and re-layouts: 18.9 us -> 2.04 us
  between operations: 13.6 us -> 0.03 us
  starting transfers between devices: 5.21 us -> 0 us
    pallas_call x0 -> x3, Pallas kernels: none -> 48.7 us  [the longest x1 32 us: exchange_call(): pl.pallas_call(exchange, out_shape=(jax.ShapeDtypeStruct((16, 2, 80, 256)...]
    all_to_all x3 -> x0, blocking collectives: 46.4 us -> none  [the longest x2 28.5 us: exchange_in_order(): whole = lax.all_to_all(whole, axes[k], k, k, tiled=True)]
    dot_general x5 -> x0, matrix products: 35.5 us -> none  [the longest x2 24 us: partial_spectra(): jnp.einsum('ws,cs->wc', weights, squares, precision=lax.Precision.HIGHEST)]
    another operation x3 -> x0, other arithmetic: 22.2 us -> none
    convert_element_type x2 -> x0, local copies, waits for them, and re-layouts: 13.8 us -> none  [the longest x1 13.7 us: shards(): return (stacked * stack_scale).astype(jnp.bfloat16)]
    ppermute x2 -> x0, starting transfers between devices: 5.21 us -> none  [shifted(): return lax.ppermute(block, axis, route)]
    unnamed x6, local copies, waits for them, and re-layouts: 0.01 us -> 2.04 us
    reshape x3 -> x0, local copies, waits for them, and re-layouts: 1.62 us -> none  [the longest x2 0.92 us: exchange_in_order(): whole = blocks.reshape(*(lax.axis_size(a) for a in axes), *inside)]
  transfers between devices with their start and end apart: 3 -> 0, of which waited for: 1 -> 0; matrix products, arithmetic and copies ran while one was open for 28% -> 0% of each run, Pallas kernels for 0% -> 0%
where the time goes in v1:
time: 51 us; the launch traced here: 50.7 us
  Pallas kernels  48.7 us (95%)
  local copies, waits for them, and re-layouts  2.04 us (4%)
    pallas_call x1, Pallas kernels, exchange_call(): pl.pallas_call(exchange, out_shape=(jax.ShapeDtypeStruct((16, 2, 80, 256)...  32 us
    pallas_call x1, Pallas kernels, local_call(): pl.pallas_call(local_sums, out_shape=jax.ShapeDtypeStruct((2, 88, 512), F...  9.4 us
    pallas_call x1, Pallas kernels, stack_call(): pl.pallas_call(stack_group, out_shape=jax.ShapeDtypeStruct((2, NB, 256, 5...  7.31 us
    unnamed x6, local copies, waits for them, and re-layouts  2.04 us

profile of v1, /device:TPU:1, one launch (start us, length us, event | category | flops | bytes accessed | tf_op | source)
XLA Modules:
  0.0 50.7 jit_solution(391855591233756010)
XLA Ops:
  0.0 0.0 copy-start.1
  0.0 0.7 %copy-done.1 = s32[32]{0:T(128)S(1)} copy-done((s32[32]{0:T(128)S(1)}, s32[32]{0:T(128)}, u32[]{:S(2)}) %copy-start.1) | copy-done | bytes 152
  0.7 0.0 copy-start.2
  0.7 0.7 %copy-done.2 = s32[20]{0:T(128)S(1)} copy-done((s32[20]{0:T(128)S(1)}, s32[20]{0:T(128)}, u32[]{:S(2)}) %copy-start.2) | copy-done | bytes 104
  1.3 9.4 %local_sums.1.part = f32[2,88,512]{2,1,0:T(8,128)S(1)} custom-call(bf16[15000,512]{1,0:T(8,128)(2,1)} %bitcast.2, s32[32]{0:T(128)S(1)} %copy-done.1, s32[20]{0:T(128)S(1)} %copy-done.2), custom_call_target="tpu_custom_call" | custom-call | tf_op jit(solution)/shard_map/local_sums/pallas_call | solution.py:149
  10.7 0.0 copy-start
  10.7 0.7 %copy-done = f32[2,88,512]{2,1,0:T(8,128)} copy-done((f32[2,88,512]{2,1,0:T(8,128)}, f32[2,88,512]{2,1,0:T(8,128)S(1)}, u32[]{:S(2)}) %copy-start) | copy-done | bytes 360472
  11.5 32.0 %exchange.1 = (bf16[16,2,80,256]{3,2,1,0:T(8,128)(2,1)}, bf16[8,2,80,256]{3,2,1,0:T(8,128)(2,1)}) custom-call(f32[2,88,512]{2,1,0:T(8,128)} %copy-done, s32[1,512]{1,0:T(1,128)} %bitcast.3), custom_call_target="tpu_custom_call" | custom-call | tf_op jit(solution)/shard_map/exchange/pallas_call | solution.py:328
  43.4 7.3 %stack.1 = bf16[2,20,256,512]{3,2,1,0:T(8,128)(2,1)} custom-call(bf16[16,2,80,256]{3,2,1,0:T(8,128)(2,1)} %get-tuple-element.7.gi, bf16[8,2,80,256]{3,2,1,0:T(8,128)(2,1)} %get-tuple-element.8.gj), custom_call_target="tpu_custom_call" | custom-call | tf_op jit(solution)/shard_map/stack/pallas_call | solution.py:368
Async XLA Ops:
  0.0 0.7 %copy-start.1 = (s32[32]{0:T(128)S(1)}, s32[32]{0:T(128)}, u32[]{:S(2)}) copy-start(s32[32]{0:T(128)} %offs.1) | copy-start | bytes 388
  0.7 0.7 %copy-start.2 = (s32[20]{0:T(128)S(1)}, s32[20]{0:T(128)}, u32[]{:S(2)}) copy-start(s32[20]{0:T(128)} %bins_ref.1) | copy-start | bytes 244
  10.7 0.7 %copy-start = (f32[2,88,512]{2,1,0:T(8,128)}, f32[2,88,512]{2,1,0:T(8,128)S(1)}, u32[]{:S(2)}) copy-start(f32[2,88,512]{2,1,0:T(8,128)S(1)} %local_sums.1.part) | copy-start | bytes 1081348

commit v2 on v1

v2 whole, which is shorter than its diff:
```python
import functools
import math

import jax
import jax.numpy as jnp
from jax import lax
from jax.experimental import pallas as pl
from jax.experimental.pallas import tpu as pltpu
from jax.sharding import PartitionSpec as P

L = 15000
NB = 20
HOP = L // 2
TWO_PI = 2.0 * math.pi
FLOOR = 0.7
WIN = 32
STEP = 1024
CHUNKS = 15
ROWS = 40
AHEAD = 6
F32 = jnp.float32
BF16 = jnp.bfloat16


def bin_rows(bins):
    row = lax.broadcasted_iota(jnp.int32, (24, 128), 0)
    out = jnp.zeros((24, 128), jnp.int32)
    for b in range(NB):
        hit = row == b
        if b >= 16:
            hit = hit | (row == b + 4)
        out = jnp.where(hit, bins[b], out)
    return out.astype(F32)


def turned(turns):
    whole = jnp.floor(turns * (1.0 / L))
    rest = turns - whole * float(L)
    rest = jnp.where(rest < 0.0, rest + float(L), rest)
    rest = jnp.where(rest >= float(L), rest - float(L), rest)
    angle = rest * (TWO_PI / L)
    return jnp.cos(angle), jnp.sin(angle)


def start_state(bins, first):
    lane = lax.broadcasted_iota(jnp.int32, (24, 128), 1)
    row = lax.broadcasted_iota(jnp.int32, (24, 128), 0)
    place = (lane + (first + L)).astype(F32)
    quarter = jnp.where(row >= 20, float(L // 4), 0.0)
    cosine, sine = turned(bins * place + quarter)
    scale = 1.0 / math.sqrt(L)
    return cosine * scale, -sine * scale


def turn_on(state, step):
    v, q = state
    c, s = step
    return v * c + q * s, q * c - v * s


def table_rows(state, keep):
    v, q = state
    rows = jnp.concatenate([v[:16], q[:16], v[16:]], axis=0)
    return rows if keep is None else jnp.where(keep, rows, 0.0)


def regroup():
    d = lax.broadcasted_iota(jnp.int32, (80, 80), 0)
    s = lax.broadcasted_iota(jnp.int32, (80, 80), 1)
    p, w = (d >> 3) & 1, (d >> 2) & 1
    b = (d >> 4) * 4 + (d & 3)
    source = w * ROWS + jnp.where(b < 16, p * 16 + b, 32 + p * 4 + (b - 16))
    return jnp.where(s == source, 1.0, 0.0).astype(BF16)


def front(
    x_hbm, offs_hbm, bins_hbm, dead_hbm, gi, gj,
    xbuf, tab, offs, bins_ref, dead, own, sums, back, recv,
    x_sems, small_sems, send_sems, back_sems, i_sems, j_sems,
):
    c = lax.axis_index("chan")
    t = lax.axis_index("tm")
    z, xl = c // 2, c % 2
    y, xh, core = t // 4, (t // 2) % 2, t % 2
    sent = []

    def send(source, target, recv_sem, device):
        copy = pltpu.make_async_remote_copy(
            src_ref=source,
            dst_ref=target,
            send_sem=send_sems.at[len(sent)],
            recv_sem=recv_sem,
            device_id=device,
            device_id_type=pl.DeviceIdType.MESH,
        )
        copy.start()
        sent.append(copy)
        return copy

    def block_of(yy, hi, k):
        return 4 * (yy % 4) + 2 * hi + k

    up, down = (c, block_of(y + 1, xh, core)), (c, block_of(y + 3, xh, core))
    across, other = (c, block_of(y, 1 - xh, core)), (c, block_of(y, xh, 1 - core))
    z_up, z_down = ((c + 2) % 8, t), ((c + 6) % 8, t)
    previous, following = (c, (t + 15) % 16), (c, (t + 1) % 16)

    barrier = pltpu.get_barrier_semaphore()
    sources = [up, down, across, other, z_up, z_down, following]
    sources += [(2 * y + xh, block_of(2 * y + 6 - z, hi, k)) for hi in range(2) for k in range(2)]
    for device in sources:
        pl.semaphore_signal(
            barrier, inc=1, device_id=device, device_id_type=pl.DeviceIdType.MESH
        )

    small = [
        pltpu.make_async_copy(src, dst, small_sems.at[n])
        for n, (src, dst) in enumerate(((offs_hbm, offs), (bins_hbm, bins_ref), (dead_hbm, dead)))
    ]
    for copy in small:
        copy.start()

    def chunk_copy(g):
        rows = STEP if isinstance(g, jax.Array) or g < CHUNKS - 1 else L - STEP * (CHUNKS - 1)
        at = pl.ds(pl.multiple_of(g * STEP, STEP), rows)
        return pltpu.make_async_copy(x_hbm.at[at], xbuf.at[at], x_sems.at[g])

    tail = (L // 16) * 16
    for g in range(AHEAD):
        chunk_copy(g).start()
    xbuf[pl.ds(tail, CHUNKS * STEP - tail)] = jnp.zeros((CHUNKS * STEP - tail, 512), BF16)
    own[...] = jnp.zeros_like(own)
    back[...] = jnp.zeros_like(back)
    sums[...] = jnp.zeros_like(sums)
    for copy in small:
        copy.wait()

    before = 2 * jnp.maximum(t - 1, 0)
    off0, off1 = offs[2 * t], offs[2 * t + 1]
    boff0, boff1 = offs[before], offs[before + 1]
    a0, a1 = off0, HOP + off1
    e0, e1 = boff0, HOP + boff1
    bins = bin_rows(bins_ref)
    step = turned(bins * 128.0)

    low = jnp.zeros((16, STEP), jnp.int32)
    high = jnp.zeros((16, STEP), jnp.int32)
    row = lax.broadcasted_iota(jnp.int32, (16, STEP), 0)
    for r, (lo, hi) in enumerate(((a0, L), (a1, L), (0, e0), (0, e1))):
        low = jnp.where(row == r, lo, low)
        high = jnp.where(row == r, hi, high)
    inner = lax.broadcasted_iota(jnp.int32, (16, STEP), 1)
    lane = lax.broadcasted_iota(jnp.int32, (ROWS, 128), 1)

    def chunk(g, slot, states, limits, targets, energies):
        states = list(states)
        tables = len(limits)
        height = 48 if tables == 1 else 80
        for k in range(STEP // 128):
            place = lane + (g * STEP + k * 128)
            rows = []
            for n, limit in enumerate(limits):
                keep = None
                if limit is not None:
                    keep = place >= limit[1] if limit[0] else place < limit[1]
                rows.append(table_rows(states[n], keep))
                states[n] = turn_on(states[n], step)
            if tables == 1:
                rows.append(jnp.zeros((8, 128), F32))
            tab[slot, 0:height, k * 128 : (k + 1) * 128] = jnp.concatenate(rows, axis=0).astype(BF16)
        x = xbuf[pl.ds(pl.multiple_of(g * STEP, STEP), STEP), :]
        raw = jnp.dot(tab[slot, 0:height, :], x, preferred_element_type=F32)
        for n, target in enumerate(targets):
            target[0:ROWS] += raw[n * ROWS : (n + 1) * ROWS]
        if energies:
            place = inner + g * STEP
            mask = jnp.where((place >= low) & (place < high), 1.0, 0.0).astype(BF16)
            sums[...] += jnp.dot(mask, x * x, preferred_element_type=F32)[0:8]
        return tuple(states)

    own0, own1 = own.at[0], own.at[1]
    back0, back1 = back.at[0], back.at[1]
    states = (start_state(bins, L - e0), start_state(bins, L - e1))
    for g in range(4):
        chunk_copy(g).wait()
        if g + AHEAD < CHUNKS:
            chunk_copy(g + AHEAD).start()
        states = chunk(g, g % 2, states, ((False, e0), None), (back0, back1), True)
    back[0, 40:41] = sums[2:3]
    pl.semaphore_wait(barrier, len(sources))
    early = send(back.at[0], recv.at[0], back_sems.at[0], previous)
    states = states[1:]
    s_own0 = start_state(bins, -a0)
    s_own1 = start_state(bins, 7 * STEP - a1)
    chunk_copy(4).wait()
    for g in range(4 + AHEAD, CHUNKS):
        chunk_copy(g).start()
    states = chunk(4, 0, states, ((False, e1),), (back1,), True)

    def pair(i, states):
        for k in range(2):
            chunk_copy(5 + 2 * i + k).wait()
        for k in range(2):
            states = chunk(5 + 2 * i + k, 1 - k, states, ((False, e1),), (back1,), True)
        return states

    lax.fori_loop(0, 3, pair, states)
    back[1, 40:41] = sums[3:4]
    late = send(back.at[1], recv.at[1], back_sems.at[1], previous)

    states = chunk(0, 0, (s_own0,), ((True, a0),), (own0,), False)

    def pair_own(i, states):
        for k in range(2):
            states = chunk(1 + 2 * i + k, 1 - k, states, ((True, a0),), (own0,), False)
        return states

    states = lax.fori_loop(0, 3, pair_own, states)
    for g in range(11, CHUNKS):
        chunk_copy(g).wait()
    both = (None, (True, a1))
    def pair_both(i, states):
        for k in range(2):
            states = chunk(7 + 2 * i + k, k, states, both, (own0, own1), False)
        return states

    def pair_last(i, states):
        for k in range(2):
            states = chunk(11 + 2 * i + k, k, states, both, (own0, own1), True)
        return states

    states = lax.fori_loop(0, 2, pair_both, states + (s_own1,))
    lax.fori_loop(0, 2, pair_last, states)

    matrix = regroup()
    alive = 1.0 - dead[...].astype(F32)
    early.wait_recv()
    late.wait_recv()
    white = []
    for w in range(2):
        more = jnp.where(t == 15, 0.0, recv[w])
        raw = own[w, 0:ROWS] + more[0:ROWS]
        energy = sums[w : w + 1] + more[40:41]
        spectra = raw / jnp.sqrt(energy / L + 1e-06)
        level = jnp.sum(spectra * spectra, axis=0, keepdims=True) * (1.0 / NB)
        white.append(spectra * (alive / jnp.sqrt(jnp.maximum(level, FLOOR))))
    white = jnp.concatenate(white, axis=0).astype(BF16)
    ordered = jnp.dot(matrix, white, preferred_element_type=F32).astype(BF16)
    for h in range(2):
        gi[t, h] = ordered[:, h * 256 : (h + 1) * 256]

    def give(block, h, device):
        send(gi.at[block, h], gi.at[block, h], i_sems.at[block, h], device)

    def got(block, h):
        pltpu.make_async_copy(gi.at[block, h], gi.at[block, h], i_sems.at[block, h]).wait()

    def pass_j(q, s, device):
        send(gj.at[q, s], gj.at[q, s], j_sems.at[q, s], device)

    def got_j(q, s):
        pltpu.make_async_copy(gj.at[q, s], gj.at[q, s], j_sems.at[q, s]).wait()

    halves = range(2)
    for h in halves:
        give(t, h, across)
    for lo in halves:
        for h in halves:
            send(
                gi.at[t, h],
                gj.at[t // 2, core],
                j_sems.at[t // 2, core],
                (2 * ((2 * z + 6 - y) % 4) + lo, block_of(z, xl, h)),
            )
    for h in halves:
        give(t, h, up)
        give(t, h, down)
    for h in halves:
        give(t, h, other)

    near = block_of(y, 1 - xh, core)
    below, above = block_of(y + 3, xh, core), block_of(y + 1, xh, core)
    far = block_of(y + 2, xh, core)
    near_below, near_above = block_of(y + 3, 1 - xh, core), block_of(y + 1, 1 - xh, core)
    near_far = block_of(y + 2, 1 - xh, core)

    got(below, 0)
    give(below, 0, up)
    got(above, 1)
    give(above, 1, down)
    for h in halves:
        got(near, h)
        give(near, h, up)
        give(near, h, down)
    q_own = [2 * ((2 * y + 6 - z) % 4) + hi for hi in range(2)]
    q_low = [2 * ((2 * y + 7 - z) % 4) + hi for hi in range(2)]
    q_high = [2 * ((2 * y + 5 - z) % 4) + hi for hi in range(2)]
    q_far = [2 * ((2 * y + 8 - z) % 4) + hi for hi in range(2)]
    for q in q_own:
        for s in halves:
            got_j(q, s)
            pass_j(q, s, z_up)
            pass_j(q, s, z_down)
    got(below, 1)
    got(above, 0)
    for block in (below, above, near):
        for h in halves:
            give(block, h, other)
    got(near_below, 0)
    give(near_below, 0, up)
    got(near_above, 1)
    give(near_above, 1, down)
    for q_l, q_h in zip(q_low, q_high):
        got_j(q_l, 0)
        pass_j(q_l, 0, z_up)
        got_j(q_h, 1)
        pass_j(q_h, 1, z_down)
    got(near_below, 1)
    got(near_above, 0)
    for block in (near_below, near_above):
        for h in halves:
            give(block, h, other)
    for block in (far, near_far):
        for h in halves:
            got(block, h)
            give(block, h, other)
    for q_l, q_h in zip(q_low, q_high):
        got_j(q_l, 1)
        got_j(q_h, 0)
    for q in q_far:
        for s in halves:
            got_j(q, s)
    for yy in range(4):
        for hi in range(2):
            for h in halves:
                got(block_of(yy, hi, 1 - core), h)
    for copy in sent:
        copy.wait_send()


N_SENDS = 48


def front_call(x, offsets, band_bins, dead):
    anywhere = pl.BlockSpec(memory_space=pltpu.HBM)
    vmem = pl.BlockSpec(memory_space=pltpu.VMEM)
    return pl.pallas_call(
        front,
        out_shape=(
            jax.ShapeDtypeStruct((16, 2, 80, 256), BF16),
            jax.ShapeDtypeStruct((8, 2, 80, 256), BF16),
        ),
        in_specs=[anywhere] * 4,
        out_specs=(vmem, vmem),
        scratch_shapes=[
            pltpu.VMEM((CHUNKS * STEP, 512), BF16),
            pltpu.VMEM((2, 80, STEP), BF16),
            pltpu.SMEM((32,), jnp.int32),
            pltpu.SMEM((NB,), jnp.int32),
            pltpu.VMEM((1, 512), jnp.int32),
            pltpu.VMEM((2, ROWS, 512), F32),
            pltpu.VMEM((8, 512), F32),
            pltpu.VMEM((2, 48, 512), F32),
            pltpu.VMEM((2, 48, 512), F32),
            pltpu.SemaphoreType.DMA((CHUNKS,)),
            pltpu.SemaphoreType.DMA((3,)),
            pltpu.SemaphoreType.DMA((N_SENDS,)),
            pltpu.SemaphoreType.DMA((2,)),
            pltpu.SemaphoreType.DMA((16, 2)),
            pltpu.SemaphoreType.DMA((8, 2)),
        ],
        compiler_params=pltpu.CompilerParams(
            collective_id=0, has_side_effects=True, vmem_limit_bytes=48 << 20
        ),
        name="front",
    )(x, offsets, band_bins, dead)


def stack_group(gi, gj, out, lhs):
    at_rows = pl.ds(pl.multiple_of(pl.program_id(0) * 16, 16), 16)
    xj = gj[:, :, at_rows, :].reshape(16, 16, 256).astype(F32)
    flipped = jnp.concatenate([-xj[:, 8:], xj[:, :8]], axis=1)
    bin_of = lax.broadcasted_iota(jnp.int32, (256, 256), 1) & 3
    for s, rows in enumerate((xj, flipped)):
        turned_rows = rows.reshape(256, 256).T
        for b in range(4):
            at = (s * 4 + b) * 256
            lhs[at : at + 256] = jnp.where(bin_of == b, turned_rows, 0.0).astype(BF16)
    scale = 1.0 / math.sqrt(WIN)
    for h in range(2):
        right = gi[:, h, at_rows, :].reshape(256, 256)
        made = jnp.dot(lhs[...], right, preferred_element_type=F32) * scale
        out[:, :, :, h * 256 : (h + 1) * 256] = made.astype(BF16).reshape(2, 4, 256, 256)


def stack_call(gi, gj):
    vmem = pl.BlockSpec(memory_space=pltpu.VMEM)
    return pl.pallas_call(
        stack_group,
        out_shape=jax.ShapeDtypeStruct((2, NB, 256, 512), BF16),
        grid=(5,),
        in_specs=[vmem, vmem],
        out_specs=pl.BlockSpec((2, 4, 256, 512), lambda g: (0, g, 0, 0)),
        scratch_shapes=[pltpu.VMEM((2048, 256), BF16)],
        compiler_params=pltpu.CompilerParams(vmem_limit_bytes=32 << 20),
        name="stack",
    )(gi, gj)


def shards(recording, offsets, band_bins, dead_flags):
    placed = [
        pltpu.with_memory_space_constraint(a, pltpu.HBM)
        for a in (recording.T, offsets, band_bins, dead_flags.reshape(1, -1))
    ]
    gi, gj = front_call(*placed)
    return stack_call(gi, gj)


def solution(mesh):
    return jax.shard_map(
        shards,
        mesh=mesh,
        in_specs=(P("chan", "tm"), P(), P(), P("chan")),
        out_specs=P(None, None, "tm", "chan"),
        check_vma=False,
    )
```

time: 51 us -> 42.1 us (0.83)
  Pallas kernels: 48.7 us -> 41.6 us
  local copies, waits for them, and re-layouts: 2.04 us -> 0 us
    pallas_call x2 -> x1, Pallas kernels: 41.4 us -> 35.4 us  [front_call(): pl.pallas_call(front, out_shape=(jax.ShapeDtypeStruct((16, 2, 80, 256), B...]
    unnamed x6 -> x0, local copies, waits for them, and re-layouts: 2.04 us -> none
    pallas_call x1, Pallas kernels: 7.31 us -> 6.25 us  [stack_call(): pl.pallas_call(stack_group, out_shape=jax.ShapeDtypeStruct((2, NB, 256, 5...]
where the time goes in v2:
time: 42.1 us; the launch traced here: 41.6 us
  Pallas kernels  41.6 us (99%)
    pallas_call x1, Pallas kernels, front_call(): pl.pallas_call(front, out_shape=(jax.ShapeDtypeStruct((16, 2, 80, 256), B...  35.4 us
    pallas_call x1, Pallas kernels, stack_call(): pl.pallas_call(stack_group, out_shape=jax.ShapeDtypeStruct((2, NB, 256, 5...  6.25 us

profile of v2, /device:TPU:1, one launch (start us, length us, event | category | flops | bytes accessed | tf_op | source)
XLA Modules:
  0.0 41.6 jit_solution(798901803597959278)
XLA Ops:
  0.0 35.4 %front.1 = (bf16[16,2,80,256]{3,2,1,0:T(8,128)(2,1)S(1)}, bf16[8,2,80,256]{3,2,1,0:T(8,128)(2,1)S(1)}) custom-call(bf16[15000,512]{1,0:T(8,128)(2,1)} %bitcast.2, s32[32]{0:T(128)} %offs_hbm.1, s32[20]{0:T(128)} %bins_hbm.1, s32[1,512]{1,0:T(1,128)} %bitcast.3), custom_call_target="tpu_custom_call" | custom-call | tf_op jit(solution)/shard_map/front/pallas_call | solution.py:347
  35.4 6.2 %stack.1 = bf16[2,20,256,512]{3,2,1,0:T(8,128)(2,1)} custom-call(bf16[16,2,80,256]{3,2,1,0:T(8,128)(2,1)S(1)} %get-tuple-element.7.gi, bf16[8,2,80,256]{3,2,1,0:T(8,128)(2,1)S(1)} %get-tuple-element.8.gj), custom_call_target="tpu_custom_call" | custom-call | tf_op jit(solution)/shard_map/stack/pallas_call | solution.py:398

commit v3 on v2

--- a/solution.py
+++ b/solution.py
@@ -105,14 +105,6 @@
     z_up, z_down = ((c + 2) % 8, t), ((c + 6) % 8, t)
     previous, following = (c, (t + 15) % 16), (c, (t + 1) % 16)
 
-    barrier = pltpu.get_barrier_semaphore()
-    sources = [up, down, across, other, z_up, z_down, following]
-    sources += [(2 * y + xh, block_of(2 * y + 6 - z, hi, k)) for hi in range(2) for k in range(2)]
-    for device in sources:
-        pl.semaphore_signal(
-            barrier, inc=1, device_id=device, device_id_type=pl.DeviceIdType.MESH
-        )
-
     small = [
         pltpu.make_async_copy(src, dst, small_sems.at[n])
         for n, (src, dst) in enumerate(((offs_hbm, offs), (bins_hbm, bins_ref), (dead_hbm, dead)))
@@ -128,6 +120,16 @@
     tail = (L // 16) * 16
     for g in range(AHEAD):
         chunk_copy(g).start()
+
+    barrier = pltpu.get_barrier_semaphore()
+    side = (2 * z + 1 - xl, t)
+    sources = [up, down, across, other, z_up, z_down, side, following]
+    sources += [(2 * y + xh, block_of(2 * y + 6 - z, xl, k)) for k in range(2)]
+    for device in sources:
+        pl.semaphore_signal(
+            barrier, inc=1, device_id=device, device_id_type=pl.DeviceIdType.MESH
+        )
+
     xbuf[pl.ds(tail, CHUNKS * STEP - tail)] = jnp.zeros((CHUNKS * STEP - tail, 512), BF16)
     own[...] = jnp.zeros_like(own)
     back[...] = jnp.zeros_like(back)
@@ -262,27 +264,28 @@
         pltpu.make_async_copy(gj.at[q, s], gj.at[q, s], j_sems.at[q, s]).wait()
 
     halves = range(2)
+    near = block_of(y, 1 - xh, core)
+    below, above = block_of(y + 3, xh, core), block_of(y + 1, xh, core)
+    far = block_of(y + 2, xh, core)
+    near_below, near_above = block_of(y + 3, 1 - xh, core), block_of(y + 1, 1 - xh, core)
+    near_far = block_of(y + 2, 1 - xh, core)
+    q_of = [[2 * ((2 * y + k - z) % 4) + hi for hi in (xl, 1 - xl)] for k in (6, 7, 5, 8)]
+    q_own, q_low, q_high, q_far = q_of
+
+    for h in halves:
+        send(
+            gi.at[t, h],
+            gj.at[t // 2, core],
+            j_sems.at[t // 2, core],
+            (2 * ((2 * z + 6 - y) % 4) + xh, block_of(z, xl, h)),
+        )
     for h in halves:
         give(t, h, across)
-    for lo in halves:
-        for h in halves:
-            send(
-                gi.at[t, h],
-                gj.at[t // 2, core],
-                j_sems.at[t // 2, core],
-                (2 * ((2 * z + 6 - y) % 4) + lo, block_of(z, xl, h)),
-            )
     for h in halves:
         give(t, h, up)
         give(t, h, down)
     for h in halves:
         give(t, h, other)
-
-    near = block_of(y, 1 - xh, core)
-    below, above = block_of(y + 3, xh, core), block_of(y + 1, xh, core)
-    far = block_of(y + 2, xh, core)
-    near_below, near_above = block_of(y + 3, 1 - xh, core), block_of(y + 1, 1 - xh, core)
-    near_far = block_of(y + 2, 1 - xh, core)
 
     got(below, 0)
     give(below, 0, up)
@@ -292,15 +295,11 @@
         got(near, h)
         give(near, h, up)
         give(near, h, down)
-    q_own = [2 * ((2 * y + 6 - z) % 4) + hi for hi in range(2)]
-    q_low = [2 * ((2 * y + 7 - z) % 4) + hi for hi in range(2)]
-    q_high = [2 * ((2 * y + 5 - z) % 4) + hi for hi in range(2)]
-    q_far = [2 * ((2 * y + 8 - z) % 4) + hi for hi in range(2)]
-    for q in q_own:
-        for s in halves:
-            got_j(q, s)
-            pass_j(q, s, z_up)
-            pass_j(q, s, z_down)
+    for s in halves:
+        got_j(q_own[0], s)
+        pass_j(q_own[0], s, side)
+        pass_j(q_own[0], s, z_up)
+        pass_j(q_own[0], s, z_down)
     got(below, 1)
     got(above, 0)
     for block in (below, above, near):
@@ -310,13 +309,16 @@
     give(near_below, 0, up)
     got(near_above, 1)
     give(near_above, 1, down)
-    for q_l, q_h in zip(q_low, q_high):
-        got_j(q_l, 0)
-        pass_j(q_l, 0, z_up)
-        got_j(q_h, 1)
-        pass_j(q_h, 1, z_down)
     got(near_below, 1)
     got(near_above, 0)
+    for s in halves:
+        got_j(q_own[1], s)
+        pass_j(q_own[1], s, z_up)
+        pass_j(q_own[1], s, z_down)
+    got_j(q_low[0], 0)
+    pass_j(q_low[0], 0, z_up)
+    got_j(q_high[0], 1)
+    pass_j(q_high[0], 1, z_down)
     for block in (near_below, near_above):
         for h in halves:
             give(block, h, other)
@@ -324,6 +326,10 @@
         for h in halves:
             got(block, h)
             give(block, h, other)
+    got_j(q_low[1], 0)
+    pass_j(q_low[1], 0, z_up)
+    got_j(q_high[1], 1)
+    pass_j(q_high[1], 1, z_down)
     for q_l, q_h in zip(q_low, q_high):
         got_j(q_l, 1)
         got_j(q_h, 0)
@@ -376,32 +382,53 @@
     )(x, offsets, band_bins, dead)
 
 
-def stack_group(gi, gj, out, lhs):
-    at_rows = pl.ds(pl.multiple_of(pl.program_id(0) * 16, 16), 16)
-    xj = gj[:, :, at_rows, :].reshape(16, 16, 256).astype(F32)
-    flipped = jnp.concatenate([-xj[:, 8:], xj[:, :8]], axis=1)
+def stack_all(gi, gj, out, lhs, made, sems):
     bin_of = lax.broadcasted_iota(jnp.int32, (256, 256), 1) & 3
-    for s, rows in enumerate((xj, flipped)):
+    scale = 1.0 / math.sqrt(WIN)
+
+    def left(g, s):
+        rows = gj[:, :, g * 16 : g * 16 + 16, :].reshape(16, 16, 256).astype(F32)
+        if s == 1:
+            rows = jnp.concatenate([-rows[:, 8:], rows[:, :8]], axis=1)
         turned_rows = rows.reshape(256, 256).T
         for b in range(4):
-            at = (s * 4 + b) * 256
-            lhs[at : at + 256] = jnp.where(bin_of == b, turned_rows, 0.0).astype(BF16)
-    scale = 1.0 / math.sqrt(WIN)
-    for h in range(2):
-        right = gi[:, h, at_rows, :].reshape(256, 256)
-        made = jnp.dot(lhs[...], right, preferred_element_type=F32) * scale
-        out[:, :, :, h * 256 : (h + 1) * 256] = made.astype(BF16).reshape(2, 4, 256, 256)
+            kept = jnp.where(bin_of == b, turned_rows, 0.0).astype(BF16)
+            lhs[g % 2, s, b * 256 : b * 256 + 256] = kept
+
+    copies = []
+    left(0, 0)
+    for g in range(5):
+        for s in range(2):
+            if s == 0:
+                left(g, 1)
+            elif g < 4:
+                left(g + 1, 0)
+            for h in range(2):
+                right = gi[:, h, g * 16 : g * 16 + 16, :].reshape(256, 256)
+                total = jnp.dot(lhs[g % 2, s], right, preferred_element_type=F32) * scale
+                made[s, 4 * g : 4 * g + 4, :, h * 256 : (h + 1) * 256] = total.astype(BF16).reshape(
+                    4, 256, 256
+                )
+            at = pl.ds(4 * g, 4)
+            copy = pltpu.make_async_copy(made.at[s, at], out.at[s, at], sems.at[2 * g + s])
+            copy.start()
+            copies.append(copy)
+    for copy in copies:
+        copy.wait()
 
 
 def stack_call(gi, gj):
     vmem = pl.BlockSpec(memory_space=pltpu.VMEM)
     return pl.pallas_call(
-        stack_group,
+        stack_all,
         out_shape=jax.ShapeDtypeStruct((2, NB, 256, 512), BF16),
-        grid=(5,),
         in_specs=[vmem, vmem],
-        out_specs=pl.BlockSpec((2, 4, 256, 512), lambda g: (0, g, 0, 0)),
-        scratch_shapes=[pltpu.VMEM((2048, 256), BF16)],
+        out_specs=pl.BlockSpec(memory_space=pltpu.HBM),
+        scratch_shapes=[
+            pltpu.VMEM((2, 2, 1024, 256), BF16),
+            pltpu.VMEM((2, NB, 256, 512), BF16),
+            pltpu.SemaphoreType.DMA((10,)),
+        ],
         compiler_params=pltpu.CompilerParams(vmem_limit_bytes=32 << 20),
         name="stack",
     )(gi, gj)

time: 42.1 us -> 38.4 us (0.912)
  the two profiles are of different devices: /device:TPU:1 before, /device:TPU:32 now
where the time goes in v3:
time: 38.4 us; the launch traced here: 38.3 us
  Pallas kernels  38.3 us (100%)
    pallas_call x1, Pallas kernels, front_call(): pl.pallas_call(front, out_shape=(jax.ShapeDtypeStruct((16, 2, 80, 256), B...  33.8 us
    pallas_call x1, Pallas kernels, stack_call(): pl.pallas_call(stack_all, out_shape=jax.ShapeDtypeStruct((2, NB, 256, 512...  4.5 us

profile of v3, /device:TPU:32, one launch (start us, length us, event | category | flops | bytes accessed | tf_op | source)
XLA Modules:
  0.0 38.3 jit_solution(13803660629466226342)
XLA Ops:
  0.0 33.8 %front.1 = (bf16[16,2,80,256]{3,2,1,0:T(8,128)(2,1)S(1)}, bf16[8,2,80,256]{3,2,1,0:T(8,128)(2,1)S(1)}) custom-call(bf16[15000,512]{1,0:T(8,128)(2,1)} %bitcast.2, s32[32]{0:T(128)} %offs_hbm.1, s32[20]{0:T(128)} %bins_hbm.1, s32[1,512]{1,0:T(1,128)} %bitcast.3), custom_call_target="tpu_custom_call" | custom-call | tf_op jit(solution)/shard_map/front/pallas_call | solution.py:353
  33.8 4.5 %stack.1 = bf16[2,20,256,512]{3,2,1,0:T(8,128)(2,1)} custom-call(bf16[16,2,80,256]{3,2,1,0:T(8,128)(2,1)S(1)} %get-tuple-element.7.gi, bf16[8,2,80,256]{3,2,1,0:T(8,128)(2,1)S(1)} %get-tuple-element.8.gj), custom_call_target="tpu_custom_call" | custom-call | tf_op jit(solution)/shard_map/stack/pallas_call | solution.py:422

commit v4 on v3

--- a/solution.py
+++ b/solution.py
@@ -42,14 +42,28 @@
     return jnp.cos(angle), jnp.sin(angle)
 
 
-def start_state(bins, first):
+def start_states(bins, firsts):
     lane = lax.broadcasted_iota(jnp.int32, (24, 128), 1)
     row = lax.broadcasted_iota(jnp.int32, (24, 128), 0)
-    place = (lane + (first + L)).astype(F32)
+    place = jnp.full((24, 128), 128, jnp.int32)
+    for n, first in enumerate(firsts):
+        place = jnp.where(lane == n, first + L, place)
+    turn_c, turn_s = turned(bins * place.astype(F32))
     quarter = jnp.where(row >= 20, float(L // 4), 0.0)
-    cosine, sine = turned(bins * place + quarter)
+    base_c, base_s = turned(bins * lane.astype(F32) + quarter)
     scale = 1.0 / math.sqrt(L)
-    return cosine * scale, -sine * scale
+    base_c, base_s = base_c * scale, base_s * scale
+    states = []
+    for n in range(len(firsts)):
+        c = jnp.broadcast_to(turn_c[:, n : n + 1], (24, 128))
+        s = jnp.broadcast_to(turn_s[:, n : n + 1], (24, 128))
+        states.append((base_c * c - base_s * s, -(base_s * c + base_c * s)))
+    at = len(firsts)
+    step = (
+        jnp.broadcast_to(turn_c[:, at : at + 1], (24, 128)),
+        jnp.broadcast_to(turn_s[:, at : at + 1], (24, 128)),
+    )
+    return states, step
 
 
 def turn_on(state, step):
@@ -143,7 +157,7 @@
     a0, a1 = off0, HOP + off1
     e0, e1 = boff0, HOP + boff1
     bins = bin_rows(bins_ref)
-    step = turned(bins * 128.0)
+    starts, step = start_states(bins, (L - e0, L - e1, -a0, 4 * STEP - a1))
 
     low = jnp.zeros((16, STEP), jnp.int32)
     high = jnp.zeros((16, STEP), jnp.int32)
@@ -157,7 +171,7 @@
     def chunk(g, slot, states, limits, targets, energies):
         states = list(states)
         tables = len(limits)
-        height = 48 if tables == 1 else 80
+        height = 80 if tables == 2 else 128
         for k in range(STEP // 128):
             place = lane + (g * STEP + k * 128)
             rows = []
@@ -167,7 +181,7 @@
                     keep = place >= limit[1] if limit[0] else place < limit[1]
                 rows.append(table_rows(states[n], keep))
                 states[n] = turn_on(states[n], step)
-            if tables == 1:
+            if tables == 3:
                 rows.append(jnp.zeros((8, 128), F32))
             tab[slot, 0:height, k * 128 : (k + 1) * 128] = jnp.concatenate(rows, axis=0).astype(BF16)
         x = xbuf[pl.ds(pl.multiple_of(g * STEP, STEP), STEP), :]
@@ -182,56 +196,44 @@
 
     own0, own1 = own.at[0], own.at[1]
     back0, back1 = back.at[0], back.at[1]
-    states = (start_state(bins, L - e0), start_state(bins, L - e1))
+    states = tuple(starts[:3])
+    first_limits = ((False, e0), None, (True, a0))
     for g in range(4):
         chunk_copy(g).wait()
         if g + AHEAD < CHUNKS:
             chunk_copy(g + AHEAD).start()
-        states = chunk(g, g % 2, states, ((False, e0), None), (back0, back1), True)
+        states = chunk(g, g % 2, states, first_limits, (back0, back1, own0), True)
     back[0, 40:41] = sums[2:3]
     pl.semaphore_wait(barrier, len(sources))
     early = send(back.at[0], recv.at[0], back_sems.at[0], previous)
-    states = states[1:]
-    s_own0 = start_state(bins, -a0)
-    s_own1 = start_state(bins, 7 * STEP - a1)
+    states = states[1:] + (starts[3],)
+    limits = ((False, e1), None, (True, a1))
+    targets = (back1, own0, own1)
     chunk_copy(4).wait()
     for g in range(4 + AHEAD, CHUNKS):
         chunk_copy(g).start()
-    states = chunk(4, 0, states, ((False, e1),), (back1,), True)
+    states = chunk(4, 0, states, limits, targets, True)
 
     def pair(i, states):
         for k in range(2):
             chunk_copy(5 + 2 * i + k).wait()
         for k in range(2):
-            states = chunk(5 + 2 * i + k, 1 - k, states, ((False, e1),), (back1,), True)
+            states = chunk(5 + 2 * i + k, 1 - k, states, limits, targets, True)
         return states
 
-    lax.fori_loop(0, 3, pair, states)
+    states = lax.fori_loop(0, 3, pair, states)
     back[1, 40:41] = sums[3:4]
     late = send(back.at[1], recv.at[1], back_sems.at[1], previous)
 
-    states = chunk(0, 0, (s_own0,), ((True, a0),), (own0,), False)
-
-    def pair_own(i, states):
-        for k in range(2):
-            states = chunk(1 + 2 * i + k, 1 - k, states, ((True, a0),), (own0,), False)
-        return states
-
-    states = lax.fori_loop(0, 3, pair_own, states)
+    states = states[1:]
     for g in range(11, CHUNKS):
         chunk_copy(g).wait()
-    both = (None, (True, a1))
-    def pair_both(i, states):
-        for k in range(2):
-            states = chunk(7 + 2 * i + k, k, states, both, (own0, own1), False)
-        return states
 
     def pair_last(i, states):
         for k in range(2):
-            states = chunk(11 + 2 * i + k, k, states, both, (own0, own1), True)
+            states = chunk(11 + 2 * i + k, k, states, (None, (True, a1)), (own0, own1), True)
         return states
 
-    states = lax.fori_loop(0, 2, pair_both, states + (s_own1,))
     lax.fori_loop(0, 2, pair_last, states)
 
     matrix = regroup()
@@ -360,7 +362,7 @@
         out_specs=(vmem, vmem),
         scratch_shapes=[
             pltpu.VMEM((CHUNKS * STEP, 512), BF16),
-            pltpu.VMEM((2, 80, STEP), BF16),
+            pltpu.VMEM((2, 128, STEP), BF16),
             pltpu.SMEM((32,), jnp.int32),
             pltpu.SMEM((NB,), jnp.int32),
             pltpu.VMEM((1, 512), jnp.int32),

time: 38.4 us -> 36 us (0.938)
  the two profiles are of different devices: /device:TPU:32 before, /device:TPU:1 now
where the time goes in v4:
time: 36 us; the launch traced here: 35.9 us
  Pallas kernels  35.9 us (100%)
    pallas_call x1, Pallas kernels, front_call(): pl.pallas_call(front, out_shape=(jax.ShapeDtypeStruct((16, 2, 80, 256), B...  31.4 us
    pallas_call x1, Pallas kernels, stack_call(): pl.pallas_call(stack_all, out_shape=jax.ShapeDtypeStruct((2, NB, 256, 512...  4.5 us

profile of v4, /device:TPU:1, one launch (start us, length us, event | category | flops | bytes accessed | tf_op | source)
XLA Modules:
  0.0 35.9 jit_solution(15248964572563886064)
XLA Ops:
  0.0 31.4 %front.1 = (bf16[16,2,80,256]{3,2,1,0:T(8,128)(2,1)S(1)}, bf16[8,2,80,256]{3,2,1,0:T(8,128)(2,1)S(1)}) custom-call(bf16[15000,512]{1,0:T(8,128)(2,1)} %bitcast.2, s32[32]{0:T(128)} %offs_hbm.1, s32[20]{0:T(128)} %bins_hbm.1, s32[1,512]{1,0:T(1,128)} %bitcast.3), custom_call_target="tpu_custom_call" | custom-call | tf_op jit(solution)/shard_map/front/pallas_call | solution.py:355
  31.4 4.5 %stack.1 = bf16[2,20,256,512]{3,2,1,0:T(8,128)(2,1)} custom-call(bf16[16,2,80,256]{3,2,1,0:T(8,128)(2,1)S(1)} %get-tuple-element.7.gi, bf16[8,2,80,256]{3,2,1,0:T(8,128)(2,1)S(1)} %get-tuple-element.8.gj), custom_call_target="tpu_custom_call" | custom-call | tf_op jit(solution)/shard_map/stack/pallas_call | solution.py:424

commit v5 on v4

--- a/solution.py
+++ b/solution.py
@@ -89,7 +89,7 @@
 
 def front(
     x_hbm, offs_hbm, bins_hbm, dead_hbm, gi, gj,
-    xbuf, tab, offs, bins_ref, dead, own, sums, back, recv,
+    xbuf, tab, offs, bins_ref, dead, own, sums, back, recv, late_out, late_in,
     x_sems, small_sems, send_sems, back_sems, i_sems, j_sems,
 ):
     c = lax.axis_index("chan")
@@ -223,7 +223,12 @@
 
     states = lax.fori_loop(0, 3, pair, states)
     back[1, 40:41] = sums[3:4]
-    late = send(back.at[1], recv.at[1], back_sems.at[1], previous)
+    late_out[...] = back[1, 0:ROWS].astype(BF16)
+    tail_rows = pl.ds(ROWS, 8)
+    late = send(late_out, late_in, back_sems.at[1], previous)
+    late_energy = send(
+        back.at[1, tail_rows], recv.at[1, tail_rows], back_sems.at[2], previous
+    )
 
     states = states[1:]
     for g in range(11, CHUNKS):
@@ -240,11 +245,12 @@
     alive = 1.0 - dead[...].astype(F32)
     early.wait_recv()
     late.wait_recv()
+    late_energy.wait_recv()
     white = []
     for w in range(2):
-        more = jnp.where(t == 15, 0.0, recv[w])
-        raw = own[w, 0:ROWS] + more[0:ROWS]
-        energy = sums[w : w + 1] + more[40:41]
+        more = late_in[...].astype(F32) if w == 1 else recv[0, 0:ROWS]
+        raw = own[w, 0:ROWS] + jnp.where(t == 15, 0.0, more)
+        energy = sums[w : w + 1] + jnp.where(t == 15, 0.0, recv[w, 40:41])
         spectra = raw / jnp.sqrt(energy / L + 1e-06)
         level = jnp.sum(spectra * spectra, axis=0, keepdims=True) * (1.0 / NB)
         white.append(spectra * (alive / jnp.sqrt(jnp.maximum(level, FLOOR))))
@@ -289,10 +295,9 @@
     for h in halves:
         give(t, h, other)
 
-    got(below, 0)
-    give(below, 0, up)
-    got(above, 1)
-    give(above, 1, down)
+    for h in halves:
+        got(above, h)
+        give(above, h, down)
     for h in halves:
         got(near, h)
         give(near, h, up)
@@ -302,17 +307,16 @@
         pass_j(q_own[0], s, side)
         pass_j(q_own[0], s, z_up)
         pass_j(q_own[0], s, z_down)
-    got(below, 1)
-    got(above, 0)
+    for h in halves:
+        got(below, h)
     for block in (below, above, near):
         for h in halves:
             give(block, h, other)
-    got(near_below, 0)
-    give(near_below, 0, up)
-    got(near_above, 1)
-    give(near_above, 1, down)
-    got(near_below, 1)
-    got(near_above, 0)
+    for h in halves:
+        got(near_above, h)
+        give(near_above, h, down)
+    for h in halves:
+        got(near_below, h)
     for s in halves:
         got_j(q_own[1], s)
         pass_j(q_own[1], s, z_up)
@@ -346,7 +350,7 @@
         copy.wait_send()
 
 
-N_SENDS = 48
+N_SENDS = 50
 
 
 def front_call(x, offsets, band_bins, dead):
@@ -370,10 +374,12 @@
             pltpu.VMEM((8, 512), F32),
             pltpu.VMEM((2, 48, 512), F32),
             pltpu.VMEM((2, 48, 512), F32),
+            pltpu.VMEM((ROWS, 512), BF16),
+            pltpu.VMEM((ROWS, 512), BF16),
             pltpu.SemaphoreType.DMA((CHUNKS,)),
             pltpu.SemaphoreType.DMA((3,)),
             pltpu.SemaphoreType.DMA((N_SENDS,)),
-            pltpu.SemaphoreType.DMA((2,)),
+            pltpu.SemaphoreType.DMA((3,)),
             pltpu.SemaphoreType.DMA((16, 2)),
             pltpu.SemaphoreType.DMA((8, 2)),
         ],

time: 36 us -> 36.5 us (1.014)
  Pallas kernels: 35.9 us -> 36.4 us
    pallas_call x1, Pallas kernels: 31.4 us -> 31.9 us  [front_call(): pl.pallas_call(front, out_shape=(jax.ShapeDtypeStruct((16, 2, 80, 256), B...]
where the time goes in v5:
time: 36.5 us; the launch traced here: 36.4 us
  Pallas kernels  36.4 us (100%)
    pallas_call x1, Pallas kernels, front_call(): pl.pallas_call(front, out_shape=(jax.ShapeDtypeStruct((16, 2, 80, 256), B...  31.9 us
    pallas_call x1, Pallas kernels, stack_call(): pl.pallas_call(stack_all, out_shape=jax.ShapeDtypeStruct((2, NB, 256, 512...  4.5 us

profile of v5, /device:TPU:1, one launch (start us, length us, event | category | flops | bytes accessed | tf_op | source)
XLA Modules:
  0.0 36.4 jit_solution(13013866679482177563)
XLA Ops:
  0.0 31.9 %front.1 = (bf16[16,2,80,256]{3,2,1,0:T(8,128)(2,1)S(1)}, bf16[8,2,80,256]{3,2,1,0:T(8,128)(2,1)S(1)}) custom-call(bf16[15000,512]{1,0:T(8,128)(2,1)} %bitcast.2, s32[32]{0:T(128)} %offs_hbm.1, s32[20]{0:T(128)} %bins_hbm.1, s32[1,512]{1,0:T(1,128)} %bitcast.3), custom_call_target="tpu_custom_call" | custom-call | tf_op jit(solution)/shard_map/front/pallas_call | solution.py:359
  31.9 4.5 %stack.1 = bf16[2,20,256,512]{3,2,1,0:T(8,128)(2,1)} custom-call(bf16[16,2,80,256]{3,2,1,0:T(8,128)(2,1)S(1)} %get-tuple-element.7.gi, bf16[8,2,80,256]{3,2,1,0:T(8,128)(2,1)S(1)} %get-tuple-element.8.gj), custom_call_target="tpu_custom_call" | custom-call | tf_op jit(solution)/shard_map/stack/pallas_call | solution.py:430
